TPU v7x, 256 devices: a whole 4x4x8 slice. The times are simulated.
256 devices in a mesh: depth: 16 (over x, z_lo), col: 16 (over z_hi, y, core).
Axes of the slice: x: 4, y: 4, z: 8 (z_hi: 2, z_lo: 4; z = z_hi * 4 + z_lo), core: 2. Of those that a mesh axis runs over, the one named last changes fastest.
Arguments:
- recorded: bfloat16 [4, 32, 2, 512, 512], P(None, 'depth', None, 'col'), may hold values from -6 to 6
- vertical: float32 [4, 512], replicated, may hold values from 0.05 to 0.8
Outputs:
- prediction: float32 [4, 2, 512, 512], P(None, None, 'col', 'depth')
All inputs are finite; a program needn't handle non-finite values.
Results may differ from a plain program's by a relative error of at most 0.01.
Values may be sent and summed in bfloat16 or wider, within the bound.
No kernel may reach another device: no remote copies, remote signals or barrier semaphores. Data moves between devices by JAX's collectives and lax.ppermute only.
A program may use at most 64 MiB of HBM per device.

v0:
```python
import jax
import jax.numpy as jnp
from jax import lax
from jax.sharding import PartitionSpec as P


def prefix(x, axis, combine, identity, reverse):
    peers, mine = (lax.axis_size(axis), lax.axis_index(axis))
    everything = lax.all_gather(x, axis)
    start = jnp.broadcast_to(jnp.asarray(identity, x.dtype), x.shape)

    def lap(k, before):
        at = peers - 1 - k if reverse else k
        reached = at > mine if reverse else at < mine
        new = combine(before, everything[at])
        return jnp.where(reached, new, before)

    return lax.fori_loop(0, peers, lap, start)


def from_behind(value, axis, steps):
    count = lax.axis_size(axis)
    initial, last = (max(0, -steps), min(count, count - steps))
    return lax.ppermute(value, axis, [(source, source + steps) for source in range(initial, last)])


def complex_product(left_side, right_side, pattern, stack_axis):
    left_real = left_side[:, :, 0]
    left_imag = left_side[:, :, 1]
    right_real = right_side[:, :, 0]
    right_imag = right_side[:, :, 1]
    real_part = jnp.einsum(
        pattern, left_real, right_real, preferred_element_type=jnp.float32
    ) - jnp.einsum(pattern, left_imag, right_imag, preferred_element_type=jnp.float32)
    imag_part = jnp.einsum(
        pattern, left_real, right_imag, preferred_element_type=jnp.float32
    ) + jnp.einsum(pattern, left_imag, right_real, preferred_element_type=jnp.float32)
    return jnp.stack([real_part, imag_part], axis=stack_axis)


def add_pair(earlier, later):
    return earlier + later


def carry_products(products):
    running = lax.cumsum(products, axis=1)
    before = prefix(running[:, -1], "depth", add_pair, jnp.zeros_like(running[:, -1]), False)
    prefix_all = running + before[:, None]
    previous = from_behind(prefix_all[:, -1], "depth", 1)
    return jnp.concatenate([previous[:, None], prefix_all[:, :-1]], axis=1).astype(jnp.bfloat16)


def shards(recorded, vertical):
    local_depths = recorded.shape[1]
    row_count = recorded.shape[3]
    depth_cells = lax.axis_size("depth") * local_depths
    depth_step = 1.0 / depth_cells
    first_row = lax.axis_index("col") * row_count
    row_wave = lax.dynamic_slice_in_dim(vertical, first_row, row_count, 1)
    depth_f = (
        lax.axis_index("depth") * local_depths + jnp.arange(local_depths, dtype=jnp.int32)
    ).astype(jnp.float32)
    phase_angle = (row_wave[:, None, :, None] + vertical[:, None, None, :]) * depth_f[
        None, :, None, None
    ]
    cosine = jnp.cos(phase_angle)
    sine_part = jnp.sin(phase_angle)
    real_in = recorded[:, :, 0].astype(jnp.float32)
    imag_in = recorded[:, :, 1].astype(jnp.float32)
    plus32 = (
        jnp.stack(
            [real_in * cosine - imag_in * sine_part, real_in * sine_part + imag_in * cosine], axis=2
        )
        * depth_step
    )
    minus_phase = (
        jnp.stack(
            [real_in * cosine + imag_in * sine_part, imag_in * cosine - real_in * sine_part], axis=2
        )
        * depth_step
    ).astype(jnp.bfloat16)
    plus_phase = plus32.astype(jnp.bfloat16)
    inner_sum = lax.cumsum(plus32, axis=1, reverse=True)
    beyond = prefix(inner_sum[:, 0], "depth", add_pair, jnp.zeros_like(inner_sum[:, 0]), True)
    suffix_all = inner_sum + beyond[:, None]
    following = from_behind(suffix_all[:, 0], "depth", -1)
    tail_sum = jnp.concatenate([suffix_all[:, 1:], following[:, None]], axis=1).astype(jnp.bfloat16)
    columns = minus_phase
    products = complex_product(
        columns, lax.all_gather(tail_sum, "col", axis=3, tiled=True), "wzrk,wzkc->wzrc", 2
    )
    lagged = carry_products(products)
    columns = plus_phase
    partial_pred = complex_product(
        columns, lax.all_gather(lagged, "col", axis=3, tiled=True), "wzrk,wzkc->wrc", 1
    )
    return lax.psum_scatter(partial_pred, "depth", scatter_dimension=3, tiled=True)


def solution(mesh):
    in_specs = (P(None, "depth", None, "col", None), P())
    out_specs = P(None, None, "col", "depth")
    return jax.shard_map(shards, mesh=mesh, in_specs=in_specs, out_specs=out_specs, check_vma=False)
```

profile of v0, /device:TPU:8, one launch (start us, length us, event | category | flops | bytes accessed | tf_op | source)
XLA Modules:
  0.0 773.7 jit_solution(15379393343514793894)
XLA Ops:
  9.2 3.1 fusion.51
  13.7 190.7 %all-gather.11.cloned.1.call-done = f32[64,1,2,32,512]{4,3,0,2,1:T(8,128)} async-done(((f32[4,1,2,32,512]{4,3,0,2,1:T(8,128)}), f32[64,1,2,32,512]{4,3,0,2,1:T(8,128)}) %all-gather.11.cloned.1.call-update) | async-done | bytes 8388624 | tf_op jit(solution)/shard_map/all_gather | solution.py:9
  204.4 20.2 %while.30 = (s32[]{:T(128)}, f32[4,2,32,512]{3,2,1,0:T(8,128)S(1)}, s32[]{:T(128)}, f32[16,4,2,32,512]{4,3,1,0,2:T(8,128)}, s32[]{:T(128)}, /*index=5*/s32[]{:T(128)}, s32[]{:T(128)}, s32[]{:T(128)}) while((s32[]{:T(128)}, f32[4,2,32,512]{3,2,1,0:T(8,128)S(1)}, s32[]{:T(128)}, f32[16,4,2,32,512]{4,3,1,0,2:T(8,128)}, s32[]{:T(128)}, ...), condition=%wide.region_2.3_spmd.clone, body=%wide.region_1.2_spmd.clone.sunk | while | flops 393224 | bytes 1573027 | solution.py:18
  205.6 1.2 add_select_fusion.4
  206.9 1.2 add_select_fusion.4
  208.2 1.2 add_select_fusion.4
  209.4 1.2 add_select_fusion.4
  210.7 1.2 add_select_fusion.4
  212.0 1.2 add_select_fusion.4
  213.2 1.2 add_select_fusion.4
  214.5 1.2 add_select_fusion.4
  215.8 1.2 add_select_fusion.4
  217.0 1.2 add_select_fusion.4
  218.3 1.2 add_select_fusion.4
  219.6 1.2 add_select_fusion.4
  220.8 1.2 add_select_fusion.4
  222.1 1.2 add_select_fusion.4
  223.3 1.2 add_select_fusion.4
  224.8 1.3 collective-permute-start
  226.1 8.4 %collective-permute-done = bf16[4,2,32,512]{3,2,0,1:T(8,128)(2,1)S(1)} collective-permute-done((bf16[4,2,32,512]{3,2,0,1:T(8,128)(2,1)S(1)}, bf16[4,2,32,512]{3,2,0,1:T(8,128)(2,1)S(1)}, u32[]{:S(2)}, u32[]{:S(2)}) %collective-permute-start) | collective-permute-done | bytes 262176 | tf_op jit(solution)/shard_map/ppermute | solution.py:24
  236.7 106.7 %all-gather.7.cloned.1.call-done = bf16[4,2,2,512,512]{4,3,1,0,2:T(8,128)(2,1)} async-done(((bf16[4,2,2,32,512]{4,3,1,0,2:T(8,128)(2,1)}), bf16[4,2,2,512,512]{4,3,1,0,2:T(8,128)(2,1)}) %all-gather.7.cloned.1.call-update) | async-done | bytes 8388624 | tf_op jit(solution)/shard_map/all_gather | solution.py:90
  343.4 3.1 fusion
  346.5 3.5 fusion.1
  353.0 183.7 %all-gather.13.cloned.1.call-done = f32[64,1,2,32,512]{4,3,1,0,2:T(8,128)} async-done(((f32[4,1,2,32,512]{4,3,1,0,2:T(8,128)}), f32[64,1,2,32,512]{4,3,1,0,2:T(8,128)}) %all-gather.13.cloned.1.call-update) | async-done | bytes 8388624 | tf_op jit(solution)/shard_map/all_gather | solution.py:9
  536.6 20.1 %while.31 = (s32[]{:T(128)}, f32[4,2,32,512]{3,2,1,0:T(8,128)S(1)}, s32[]{:T(128)}, f32[16,4,2,32,512]{4,3,1,0,2:T(8,128)}, s32[]{:T(128)}, /*index=5*/s32[]{:T(128)}) while((s32[]{:T(128)}, f32[4,2,32,512]{3,2,1,0:T(8,128)S(1)}, s32[]{:T(128)}, f32[16,4,2,32,512]{4,3,1,0,2:T(8,128)}, s32[]{:T(128)}, /*index=5*/s32[]{:T(128)}) %tuple.96), condition=%wide.region_5.6_spmd.clone, body=%wide.region_4.5_spmd.clone.sunk | while | flops 393220 | bytes 1572965 | solution.py:18
  537.9 1.2 add_select_fusion.5
  557.0 1.3 collective-permute-start.1
  558.3 5.6 collective-permute-done.1
  565.0 109.7 %all-gather.9.cloned.1.call-done = bf16[4,2,2,512,512]{4,3,1,0,2:T(8,128)(2,1)} async-done(((bf16[4,2,2,32,512]{4,3,1,0,2:T(8,128)(2,1)}), bf16[4,2,2,512,512]{4,3,1,0,2:T(8,128)(2,1)}) %all-gather.9.cloned.1.call-update) | async-done | bytes 8388624 | tf_op jit(solution)/shard_map/all_gather | solution.py:95
  674.7 3.8 slice_bitcast_fusion
  682.9 2.0 reshape.30
  685.0 80.6 %reduce-scatter.4.cloned.1.call-done = f32[32,256]{1,0:T(8,128)} async-done(((f32[512,256]{1,0:T(8,128)}), f32[32,256]{1,0:T(8,128)}) %reduce-scatter.4.cloned.1.call-update) | async-done | bytes 32784
  (57 shorter events, 36.2 us)
Async XLA Ops:
  6.5 197.9 %all-gather.11.cloned.1.call-start = ((), (), s32[]{:S(2)}) async-start(), calls=%async_computation.3 | async-start | bytes 8912896 | tf_op jit(solution)/shard_map/all_gather | solution.py:9
  13.6 329.8 %all-gather.7.cloned.1.call-start = ((), (), s32[]{:S(2)}) async-start(), calls=%async_computation.1 | async-start | bytes 8912896 | tf_op jit(solution)/shard_map/all_gather | solution.py:90
  224.8 9.7 %collective-permute-start = (bf16[4,2,32,512]{3,2,0,1:T(8,128)(2,1)S(1)}, bf16[4,2,32,512]{3,2,0,1:T(8,128)(2,1)S(1)}, u32[]{:S(2)}, u32[]{:S(2)}) collective-permute-start(bf16[4,2,32,512]{3,2,0,1:T(8,128)(2,1)S(1)} %get-tuple-element.269), channel_id=1, source_target_pairs={{16,0},{32,16},{48,32},{64,48},{80,64},{96,80},{112,96},{128,112},... | collective-permute-start | bytes 786440 | tf_op jit(solution)/shard_map/ppermute | solution.py:24
  235.4 301.2 %all-gather.13.cloned.1.call-start = ((), (), s32[]{:S(2)}) async-start(), calls=%async_computation.4 | async-start | bytes 8912896 | tf_op jit(solution)/shard_map/all_gather | solution.py:9
  343.4 6.6 copy-start
  352.9 321.8 %all-gather.9.cloned.1.call-start = ((), (), s32[]{:S(2)}) async-start(), calls=%async_computation.2 | async-start | bytes 8912896 | tf_op jit(solution)/shard_map/all_gather | solution.py:95
  557.0 6.9 collective-permute-start.1
  564.8 200.7 %reduce-scatter.4.cloned.1.call-start = ((), (), s32[]{:S(2)}) async-start(), calls=%async_computation.5 | async-start | bytes 557056
Sparse Core Ops, SparseCore 0:
  13.7 190.6 all-gather.10
  235.6 107.7 all-gather.6
  353.0 183.5 all-gather.12
  564.9 109.7 all-gather.8
  685.1 80.4 reduce-scatter.3
where the time goes:
time: 776 us; the launch traced here: 774 us
  waiting for transfers between devices  685 us (88%)
  other arithmetic  47.8 us (6%)
  between operations  13.3 us (2%)
  local copies, waits for them, and re-layouts  12.3 us (2%)
  matrix products  11.2 us (1%)
    all_gather x2, waiting for transfers between devices, prefix(): everything = lax.all_gather(x, axis)  374 us
    all_gather x1, waiting for transfers between devices, shards(): lax.all_gather(lagged, 'col', axis=3, tiled=True)  110 us
    all_gather x1, waiting for transfers between devices, shards(): lax.all_gather(tail_sum, 'col', axis=3, tiled=True)  107 us
    unnamed x6, waiting for transfers between devices  80.7 us
    select_n x32, other arithmetic, lap(): return jnp.where(reached, new, before)  39.5 us
  transfers between devices with their start and end apart: 7, of which 7 were waited for; matrix products, arithmetic and copies ran while one was open for 0% of the time, Pallas kernels for 0%

commit v1 on v0

--- a/solution.py
+++ b/solution.py
@@ -2,6 +2,11 @@
 import jax.numpy as jnp
 from jax import lax
 from jax.sharding import PartitionSpec as P
+
+
+def gather_over(x, mesh_axis, dim):
+    repeated = jnp.stack([x] * lax.axis_size(mesh_axis))
+    return jnp.concatenate(lax.all_to_all(repeated, mesh_axis, 0, 0), axis=dim)
 
 
 def prefix(x, axis, combine, identity, reverse):
@@ -86,9 +91,7 @@
     following = from_behind(suffix_all[:, 0], "depth", -1)
     tail_sum = jnp.concatenate([suffix_all[:, 1:], following[:, None]], axis=1).astype(jnp.bfloat16)
     columns = minus_phase
-    products = complex_product(
-        columns, lax.all_gather(tail_sum, "col", axis=3, tiled=True), "wzrk,wzkc->wzrc", 2
-    )
+    products = complex_product(columns, gather_over(tail_sum, "col", 3), "wzrk,wzkc->wzrc", 2)
     lagged = carry_products(products)
     columns = plus_phase
     partial_pred = complex_product(

time: 776 us -> 922 us (1.19)
  waiting for transfers between devices: 685 us -> 812 us
    all_to_all x0 -> x1, waiting for transfers between devices: none -> 126 us  [gather_over(): return jnp.concatenate(lax.all_to_all(repeated, mesh_axis, 0, 0), axis=dim)]
    all_gather x2, waiting for transfers between devices: 374 us -> 481 us  [prefix(): everything = lax.all_gather(x, axis)]
    all_gather x1 -> x0, waiting for transfers between devices: 107 us -> none  [shards(): lax.all_gather(tail_sum, 'col', axis=3, tiled=True)]
    unnamed x6 -> x5, waiting for transfers between devices: 80.7 us -> 80.8 us
where the time goes in v1:
time: 922 us; the launch traced here: 920 us
  waiting for transfers between devices  812 us (88%)
  other arithmetic  47.1 us (5%)
  local copies, waits for them, and re-layouts  20 us (2%)
  matrix products  16.2 us (2%)
  between operations  13.3 us (1%)
  starting transfers between devices  10.2 us (1%)
    all_gather x2, waiting for transfers between devices, prefix(): everything = lax.all_gather(x, axis)  481 us
    all_to_all x1, waiting for transfers between devices, gather_over(): return jnp.concatenate(lax.all_to_all(repeated, mesh_axis, 0, 0), axis=dim)  126 us
    all_gather x1, waiting for transfers between devices, shards(): lax.all_gather(lagged, 'col', axis=3, tiled=True)  110 us
    unnamed x5, waiting for transfers between devices  80.8 us
    select_n x32, other arithmetic, lap(): return jnp.where(reached, new, before)  39.5 us
  transfers between devices with their start and end apart: 7, of which 7 were waited for; matrix products, arithmetic and copies ran while one was open for 0% of the time, Pallas kernels for 0%

profile of v1, /device:TPU:8, one launch (start us, length us, event | category | flops | bytes accessed | tf_op | source)
XLA Modules:
  0.0 919.5 jit_solution(16265848408180644492)
XLA Ops:
  8.1 4.2 fusion.31
  13.7 190.8 %all-gather.8.cloned.1.call-done = f32[64,1,2,32,512]{4,3,1,0,2:T(8,128)} async-done(((f32[4,1,2,32,512]{4,3,1,0,2:T(8,128)}), f32[64,1,2,32,512]{4,3,1,0,2:T(8,128)}) %all-gather.8.cloned.1.call-update) | async-done | bytes 8388624 | tf_op jit(solution)/shard_map/all_gather | solution.py:14
  204.5 20.2 %while.30 = (s32[]{:T(128)}, f32[4,2,32,512]{3,2,1,0:T(8,128)S(1)}, s32[]{:T(128)}, f32[16,4,2,32,512]{4,3,1,0,2:T(8,128)}, s32[]{:T(128)}, /*index=5*/s32[]{:T(128)}, s32[]{:T(128)}, s32[]{:T(128)}) while((s32[]{:T(128)}, f32[4,2,32,512]{3,2,1,0:T(8,128)S(1)}, s32[]{:T(128)}, f32[16,4,2,32,512]{4,3,1,0,2:T(8,128)}, s32[]{:T(128)}, ...), condition=%wide.region_2.3_spmd.clone, body=%wide.region_1.2_spmd.clone.sunk | while | flops 393224 | bytes 1573027 | solution.py:23
  205.8 1.2 add_select_fusion.4
  207.0 1.2 add_select_fusion.4
  208.3 1.2 add_select_fusion.4
  209.6 1.2 add_select_fusion.4
  210.8 1.2 add_select_fusion.4
  212.1 1.2 add_select_fusion.4
  213.4 1.2 add_select_fusion.4
  214.6 1.2 add_select_fusion.4
  215.9 1.2 add_select_fusion.4
  217.1 1.2 add_select_fusion.4
  218.4 1.2 add_select_fusion.4
  219.7 1.2 add_select_fusion.4
  224.9 1.3 collective-permute-start
  226.2 8.4 collective-permute-done
  234.8 4.3 stack.20
  239.1 7.5 all-to-all-start
  246.7 125.9 %all-to-all-done = bf16[16,4,2,2,32,512]{5,4,2,1,3,0:T(8,128)(2,1)} async-done(((bf16[16,4,2,2,32,512]{5,4,2,1,3,0:T(8,128)(2,1)}), bf16[16,4,2,2,32,512]{5,4,2,1,3,0:T(8,128)(2,1)}, u32[]{:S(2)}, u32[]{:S(2)}) %all-to-all-start) | async-done | bytes 8388640 | tf_op jit(solution)/shard_map/all_to_all | solution.py:9
  372.7 8.3 copy.19
  380.9 3.1 fusion
  384.1 3.5 fusion.1
  390.5 290.7 %all-gather.10.cloned.1.call-done = f32[64,1,2,32,512]{4,3,1,0,2:T(8,128)} async-done(((f32[4,1,2,32,512]{4,3,1,0,2:T(8,128)}), f32[64,1,2,32,512]{4,3,1,0,2:T(8,128)}) %all-gather.10.cloned.1.call-update) | async-done | bytes 8388624 | tf_op jit(solution)/shard_map/all_gather | solution.py:14
  681.2 20.1 %while.31 = (s32[]{:T(128)}, f32[4,2,32,512]{3,2,1,0:T(8,128)S(1)}, s32[]{:T(128)}, f32[16,4,2,32,512]{4,3,1,0,2:T(8,128)}, s32[]{:T(128)}, /*index=5*/s32[]{:T(128)}) while((s32[]{:T(128)}, f32[4,2,32,512]{3,2,1,0:T(8,128)S(1)}, s32[]{:T(128)}, f32[16,4,2,32,512]{4,3,1,0,2:T(8,128)}, s32[]{:T(128)}, /*index=5*/s32[]{:T(128)}) %tuple.91), condition=%wide.region_5.6_spmd.clone, body=%wide.region_4.5_spmd.clone.sunk | while | flops 393220 | bytes 1572965 | solution.py:23
  701.6 1.3 collective-permute-start.1
  702.9 5.6 collective-permute-done.1
  709.6 109.7 %all-gather.6.cloned.1.call-done = bf16[4,2,2,512,512]{4,3,1,0,2:T(8,128)(2,1)} async-done(((bf16[4,2,2,32,512]{4,3,1,0,2:T(8,128)(2,1)}), bf16[4,2,2,512,512]{4,3,1,0,2:T(8,128)(2,1)}) %all-gather.6.cloned.1.call-update) | async-done | bytes 8388624 | tf_op jit(solution)/shard_map/all_gather | solution.py:98
  819.3 3.1 fusion.13
  822.4 3.5 fusion.12
  828.6 2.0 reshape.47
  830.7 80.7 %reduce-scatter.4.cloned.1.call-done = f32[32,256]{1,0:T(8,128)} async-done(((f32[512,256]{1,0:T(8,128)}), f32[32,256]{1,0:T(8,128)}) %reduce-scatter.4.cloned.1.call-update) | async-done | bytes 32784
  (60 shorter events, 36.6 us)
Async XLA Ops:
  6.5 198.0 %all-gather.8.cloned.1.call-start = ((), (), s32[]{:S(2)}) async-start(), calls=%async_computation.3 | async-start | bytes 8912896 | tf_op jit(solution)/shard_map/all_gather | solution.py:14
  224.9 9.7 %collective-permute-start = (bf16[4,2,32,512]{3,2,0,1:T(8,128)(2,1)S(1)}, bf16[4,2,32,512]{3,2,0,1:T(8,128)(2,1)S(1)}, u32[]{:S(2)}, u32[]{:S(2)}) collective-permute-start(bf16[4,2,32,512]{3,2,0,1:T(8,128)(2,1)S(1)} %get-tuple-element.265), channel_id=1, source_target_pairs={{16,0},{32,16},{48,32},{64,48},{80,64},{96,80},{112,96},{128,112},... | collective-permute-start | bytes 786440 | tf_op jit(solution)/shard_map/ppermute | solution.py:29
  239.1 7.5 copy-start.2
  239.1 133.6 %all-to-all-start = ((bf16[16,4,2,2,32,512]{5,4,2,1,3,0:T(8,128)(2,1)}), bf16[16,4,2,2,32,512]{5,4,2,1,3,0:T(8,128)(2,1)}, u32[]{:S(2)}, u32[]{:S(2)}) async-start(bf16[16,4,2,2,32,512]{5,4,2,1,3,0:T(8,128)(2,1)} %stack.20), calls=%async_computation | async-start | bytes 16777216 | tf_op jit(solution)/shard_map/all_to_all | solution.py:9
  246.6 434.6 %all-gather.10.cloned.1.call-start = ((), (), s32[]{:S(2)}) async-start(), calls=%async_computation.4 | async-start | bytes 8912896 | tf_op jit(solution)/shard_map/all_gather | solution.py:14
  380.9 6.6 copy-start
  390.4 428.8 %all-gather.6.cloned.1.call-start = ((), (), s32[]{:S(2)}) async-start(), calls=%async_computation.2 | async-start | bytes 8912896 | tf_op jit(solution)/shard_map/all_gather | solution.py:98
  701.6 6.9 collective-permute-start.1
  709.4 202.0 %reduce-scatter.4.cloned.1.call-start = ((), (), s32[]{:S(2)}) async-start(), calls=%async_computation.5 | async-start | bytes 557056
  819.3 6.6 copy-start.1
Sparse Core Ops, SparseCore 0:
  13.8 190.6 all-gather.7
  390.6 290.5 all-gather.9
  709.5 109.7 all-gather.5
  830.8 80.5 reduce-scatter.3
